TPU v7x, 32 devices: a whole 2x2x4 slice. The times are simulated.
32 devices in a mesh: grp: 2 (over y), doc: 4 (over x, core), voc: 4 (over z).
Axes of the slice: x: 2, y: 2, z: 4, core: 2. Of those that a mesh axis runs over, the one named last changes fastest.
Arguments:
- hidden: bfloat16 [48, 256, 768], P(('grp', 'doc')), parts along dimension 0, may hold values from -6 to 6
- lengths: int32 [48], P(('grp', 'doc')), parts along dimension 0, may hold values from 1 to 256, 3840 in all
- w_trans: bfloat16 [768, 768], replicated, may hold values from -0.21875 to 0.21875
- b_trans: float32 [768], replicated, may hold values from -3 to 3
- ln_gain: float32 [768], replicated, may hold values from 0.5 to 1.5
- ln_bias: float32 [768], replicated, may hold values from -3 to 3
- w_decode: bfloat16 [768, 30720], P(None, 'voc'), may hold values from -0.21875 to 0.21875
- b_decode: float32 [30720], P('voc'), may hold values from -5 to 5
- query_ids: int32 [2048, 32], P('grp'), parts along dimension 0, may hold values from 0 to 30719
- query_wts: int32 [2048, 32], P('grp'), parts along dimension 0, may hold values from 1 to 100
Outputs:
- scores: float32 [48, 1024], P(('grp', 'voc'), 'doc'), parts along dimension 0
There are 2 independent parts, one for each index of `grp`. A program takes and returns all parts, laid end to end along the dimension named above; an argument that names none is the same for every part. Nothing has to cross between parts.
Inputs may be any that keep to these rules, and one draw needn't show every extreme that they name: Every passage has at least one live token and the longest has exactly 256. Within each grp group the 24 lengths sum to 3840; over the whole array, which holds both groups, the sum is twice that.
All inputs are finite; a program needn't handle non-finite values.
Results may differ from a plain program's by a relative error of at most 0.0003.
Values sent between devices are 32-bit elements; how exact they have to be, the bound alone decides.
A program may use at most 64 MiB of HBM per device.

v0:
```python
import functools

import jax
import jax.numpy as jnp
from jax import lax
from jax.experimental import pallas as pl
from jax.experimental.pallas import tpu as pltpu
from jax.sharding import PartitionSpec as P

eps = 1e-06
score_scale = 1.0 / 1024.0
radix = 256
pad = 8


def tile_of(width):
    best = 128
    for tile in range(128, 1537, 128):
        if width % tile == 0:
            best = tile
    return best


def encode_kernel(
    sizes, count, tile, lens, b_trans, gain, bias, b_decode, hidden, w_trans, w_decode, ids, wts,
    out, states, mix, decoder, kept, slots, own_ids, own_wts, hi_at, lo_at, weight_at, table,
    part, parts, load_sem, state_sem, decoder_sem, doc_send, doc_recv, voc_send, voc_recv
):
    docs, vocs = sizes
    length, features = hidden.shape[0] // count, hidden.shape[1]
    width = w_decode.shape[1]
    tiles = width // tile
    slots_per, queries = own_ids.shape
    per = radix // slots_per
    leads = width // radix
    grp, doc, voc = (lax.axis_index(name) for name in ("grp", "doc", "voc"))
    mesh_ids = pl.DeviceIdType.MESH

    def state_load(p):
        rows = pl.ds(pl.multiple_of(p * length, length), length)
        return pltpu.make_async_copy(hidden.at[rows], states.at[rows], state_sem.at[p])

    def decoder_load(t):
        cut = pl.ds(pl.multiple_of(t * tile, tile), tile)
        return pltpu.make_async_copy(w_decode.at[:, cut], decoder.at[t], decoder_sem.at[t])

    mix_load = pltpu.make_async_copy(w_trans, mix, load_sem.at[0])
    mix_load.start()
    for p in range(count):
        state_load(p).start()
    rows = pl.ds(pl.multiple_of(doc * queries, queries), queries)
    loads = [
        pltpu.make_async_copy(ids.at[:, rows], own_ids, load_sem.at[1]),
        pltpu.make_async_copy(wts.at[:, rows], own_wts, load_sem.at[2]),
    ]
    for load in loads:
        load.start()
    for t in range(tiles):
        decoder_load(t).start()

    barrier = pltpu.get_barrier_semaphore()
    across = [(grp, lax.rem(doc + j, docs), voc) for j in range(1, docs)]
    along = [(grp, doc, lax.rem(voc + j, vocs)) for j in range(1, vocs)]
    for peer in across + along:
        pl.semaphore_signal(barrier, inc=1, device_id=peer, device_id_type=mesh_ids)
    mix_load.wait()

    def transform(p, _):
        state_load(p).wait()
        rows = pl.ds(pl.multiple_of(p * length, length), length)
        pre = jnp.dot(states[rows, :], mix[...], preferred_element_type=jnp.float32)
        pre = pre + b_trans[...][None]
        active = 0.5 * pre * (1.0 + lax.erf(pre * (0.5 ** 0.5)))
        centre = active - jnp.mean(active, -1, keepdims=True)
        spread = jnp.mean(centre * centre, -1, keepdims=True)
        normed = centre * lax.rsqrt(spread + eps) * gain[...][None] + bias[...][None]
        inside = lax.broadcasted_iota(jnp.int32, (length, features), 0) < lens[p]
        kept[rows, :] = jnp.where(inside, normed, normed[0:1]).astype(jnp.bfloat16)
        return 0

    lax.fori_loop(0, count, transform, 0)
    pl.semaphore_wait(barrier, len(across) + len(along))

    for load in loads:
        load.wait()
    local = own_ids[...] - voc * width
    lead = jnp.clip(local >> 8, -1, leads)
    spread_to = (
        lax.broadcasted_iota(jnp.int32, (slots_per, radix), 1) % slots_per
        == lax.broadcasted_iota(jnp.int32, (slots_per, radix), 0)
    ).astype(jnp.float32).astype(jnp.bfloat16)

    def widen(value):
        value = value.astype(jnp.float32).astype(jnp.bfloat16)
        return lax.dot_general(
            value, spread_to, (((0,), (0,)), ((), ())), preferred_element_type=jnp.float32
        )

    own = (
        lax.broadcasted_iota(jnp.int32, (queries, radix), 0) % per
        == lax.broadcasted_iota(jnp.int32, (queries, radix), 1) // slots_per
    )
    hi_at[...] = jnp.where(own, widen(lead), -1.0)
    lo_at[...] = jnp.where(own, widen(local & (radix - 1)), 0.0)
    weight_at[...] = widen(own_wts[...])

    def build(g, _):
        at = pl.ds(pl.multiple_of(g * per, per), per)
        high, weight = hi_at[at, :], weight_at[at, :]
        low = jnp.sum(lo_at[at, :], 0, keepdims=True)
        spans = leads + leads % 2
        left = jnp.concatenate(
            [jnp.where(high == float(i), weight, 0.0) for i in range(spans)], 0
        ).astype(jnp.bfloat16)
        digits = lax.broadcasted_iota(jnp.int32, (radix, radix), 0).astype(jnp.float32)
        right = jnp.where(digits == low, 1.0, 0.0).astype(jnp.bfloat16)
        made = lax.dot_general(
            left, right, (((1,), (1,)), ((), ())), preferred_element_type=jnp.float32
        )
        for i in range(leads):
            table[at, i * radix:(i + 1) * radix] = made[i * per:(i + 1) * per]
        return 0

    groups = queries // per
    inner = groups * 5 // 8 // tiles

    def share_copy(j, t):
        mine = slots.at[doc, t]
        return pltpu.make_async_remote_copy(
            src_ref=mine, dst_ref=mine, send_sem=doc_send.at[j, t], recv_sem=doc_recv.at[j, t],
            device_id=across[j], device_id_type=mesh_ids
        )

    def decode(t, _):
        decoder_load(t).wait()
        for i in range(inner):
            build(t * inner + i, 0)
        tops = []
        for p in range(count):
            logits = jnp.dot(
                kept[p * length:(p + 1) * length, :], decoder[t],
                preferred_element_type=jnp.float32
            )
            tops.append(jnp.max(logits, 0, keepdims=True))
        tops.append(jnp.zeros((pad - count, tile), jnp.float32))
        cut = pl.ds(pl.multiple_of(t * tile, tile), tile)
        best = jnp.concatenate(tops, 0) + b_decode[cut][None]
        slots[doc, t] = jnp.log1p(jnp.maximum(best, 0.0))
        for j in range(len(across)):
            share_copy(j, t).start()
        return 0

    lax.fori_loop(0, tiles, decode, 0)

    lax.fori_loop(inner * tiles, groups, build, 0)

    def arrive(t, _):
        for j in range(len(across)):
            share_copy(j, t).wait()
        return 0

    lax.fori_loop(0, tiles, arrive, 0)

    total = jnp.zeros((2 * docs * pad, queries), jnp.float32)
    for t in range(tiles):
        value = slots[:, t].reshape(docs * pad, tile)
        top = value.astype(jnp.bfloat16)
        rest = (value - top.astype(jnp.float32)).astype(jnp.bfloat16)
        pair = jnp.concatenate([top, rest], 0)
        weight = table[:, t * tile:(t + 1) * tile]
        big = weight.astype(jnp.bfloat16)
        small = (weight - big.astype(jnp.float32)).astype(jnp.bfloat16)
        for piece in (big, small):
            total = total + lax.dot_general(
                pair, piece, (((1,), (1,)), ((), ())), preferred_element_type=jnp.float32
            )
    total = (total[:docs * pad] + total[docs * pad:]) * score_scale
    part[...] = total.reshape(docs, pad, queries)

    share = docs // vocs
    copies = []
    for j, peer in enumerate(along):
        copy = pltpu.make_async_remote_copy(
            src_ref=part.at[pl.ds(peer[2] * share, share)], dst_ref=parts.at[j],
            send_sem=voc_send.at[j], recv_sem=voc_recv.at[j], device_id=peer,
            device_id_type=mesh_ids
        )
        copy.start()
        copies.append(copy)
    result = part[pl.ds(voc * share, share)]
    for j, copy in enumerate(copies):
        copy.wait()
        result = result + parts[j]
    for i in range(share):
        out[i * count:(i + 1) * count, :] = result[i, :count]


def shards(
    hidden, lengths, w_trans, b_trans, ln_gain, ln_bias, w_decode, b_decode, query_ids, query_wts
):
    docs, vocs = lax.axis_size("doc"), lax.axis_size("voc")
    count, length, features = hidden.shape
    width = w_decode.shape[1]
    tile = tile_of(width)
    tiles = width // tile
    terms = query_ids.shape[1]
    queries = query_ids.shape[0] // docs
    anywhere = pl.BlockSpec(memory_space=pl.ANY)
    inside = pl.BlockSpec(memory_space=pltpu.VMEM)
    lanes = pltpu.VMEM((queries, radix), jnp.float32)
    queue = pltpu.SemaphoreType.DMA
    return pl.pallas_call(
        functools.partial(encode_kernel, (docs, vocs), count, tile),
        out_shape=jax.ShapeDtypeStruct((docs * count // vocs, queries), jnp.float32),
        in_specs=[pl.BlockSpec(memory_space=pltpu.SMEM)] + [inside] * 4 + [anywhere] * 5,
        out_specs=inside,
        scratch_shapes=[
            pltpu.VMEM((count * length, features), jnp.bfloat16),
            pltpu.VMEM((features, features), jnp.bfloat16),
            pltpu.VMEM((tiles, features, tile), jnp.bfloat16),
            pltpu.VMEM((count * length, features), jnp.bfloat16),
            pltpu.VMEM((docs, tiles, pad, tile), jnp.float32),
            pltpu.VMEM((terms, queries), jnp.int32),
            pltpu.VMEM((terms, queries), jnp.int32),
            lanes, lanes, lanes,
            pltpu.VMEM((queries, width), jnp.float32),
            pltpu.VMEM((docs, pad, queries), jnp.float32),
            pltpu.VMEM((vocs - 1, docs // vocs, pad, queries), jnp.float32),
            queue((3,)), queue((count,)), queue((tiles,)),
            queue((docs - 1, tiles)), queue((docs - 1, tiles)),
            queue((vocs - 1,)), queue((vocs - 1,)),
        ],
        compiler_params=pltpu.CompilerParams(
            collective_id=0, has_side_effects=True, vmem_limit_bytes=60 * 1024 * 1024
        ),
    )(
        lengths, b_trans, ln_gain, ln_bias, b_decode,
        hidden.reshape(count * length, features), w_trans, w_decode, query_ids.T, query_wts.T
    )


def solution(mesh):
    return jax.shard_map(
        shards,
        mesh=mesh,
        in_specs=(
            P(("grp", "doc"), None, None),
            P(("grp", "doc")),
            P(),
            P(),
            P(),
            P(),
            P(None, "voc"),
            P("voc"),
            P("grp", None),
            P("grp", None),
        ),
        out_specs=P(("grp", "voc"), "doc"),
        check_vma=False,
    )
```

profile of v0, /device:TPU:0, one launch (start us, length us, event | category | flops | bytes accessed | tf_op | source)
XLA Modules:
  0.0 44.5 jit_solution(5031041407116833735)
XLA Ops:
  0.0 43.2 %shard_map.100 = f32[6,256]{1,0:T(8,128)} custom-call(s32[6]{0:T(128)} %lens.1, f32[768]{0:T(1024)} %b_trans.1, f32[768]{0:T(1024)} %gain.1, f32[768]{0:T(1024)} %bias.1, f32[7680]{0:T(1024)} %b_decode.1, bf16[1536,768]{1,0:T(8,128)(2,1)} %bitcast.3, bf16[768,768]{1,0:T(8,128)(2,1)} %w_trans.1, bf16[768,7680]{1,0:T(8,128)(2,1)} %w_decode.1, ...), custom_call_target="tpu_custom_call" | custom-call | tf_op jit(solution)/shard_map/pallas_call | solution.py:212
  43.2 1.3 %copy.12 = f32[6,256]{1,0:T(8,128)} copy(f32[6,256]{1,0:T(8,128)} %shard_map.100) | data formatting | bytes 12288
where the time goes:
time: 44.7 us; the launch traced here: 44.5 us
  Pallas kernels  43.2 us (97%)
  local copies, waits for them, and re-layouts  1.3 us (3%)
    pallas_call x1, Pallas kernels, shards(): pl.pallas_call(functools.partial(encode_kernel, (docs, vocs), count, tile...  43.2 us
    unnamed x1, local copies, waits for them, and re-layouts  1.3 us

commit v1 on v0

v1 whole, which is shorter than its diff:
```python
import functools

import jax
import jax.numpy as jnp
from jax import lax
from jax.experimental import pallas as pl
from jax.experimental.pallas import tpu as pltpu
from jax.sharding import PartitionSpec as P

eps = 1e-06
score_scale = 1.0 / 1024.0
radix = 256
pad = 8


def tile_of(width):
    best = 128
    for tile in range(128, 1537, 128):
        if width % tile == 0:
            best = tile
    return best


def pieces_of(tile):
    if tile < 768 or tile % 256:
        return [tile]
    first = tile // 512 * 256
    return [cut for cut in (first, tile - first - 256, 256) if cut]


def encode_kernel(
    sizes, count, tile, lens, b_trans, gain, bias, b_decode, hidden, w_trans, w_decode, ids, wts,
    out, states, mix, decoder, kept, slots, own_ids, own_wts, hi_at, lo_at, weight_at, big, small,
    part, parts, live, shift, scale, offset, floor,
    load_sem, state_sem, decoder_sem, doc_send, doc_recv, voc_send, voc_recv
):
    docs, vocs = sizes
    length, features = hidden.shape[0] // count, hidden.shape[1]
    width = w_decode.shape[1]
    tiles = width // tile
    slots_per, queries = own_ids.shape
    per = radix // slots_per
    leads = width // radix
    grp, doc, voc = (lax.axis_index(name) for name in ("grp", "doc", "voc"))
    mesh_ids = pl.DeviceIdType.MESH

    def state_load(p):
        rows = pl.ds(p * length, length)
        return pltpu.make_async_copy(hidden.at[rows], states.at[rows], state_sem.at[p])

    def decoder_load(t):
        cut = pl.ds(pl.multiple_of(t * tile, tile), tile)
        return pltpu.make_async_copy(w_decode.at[:, cut], decoder.at[t], decoder_sem.at[t])

    rows = pl.ds(pl.multiple_of(doc * queries, queries), queries)
    smalls = [
        pltpu.make_async_copy(source, target, load_sem.at[i])
        for i, (source, target) in enumerate(
            [(lens, live), (b_trans, shift), (gain, scale), (bias, offset)]
        )
    ]
    later = [
        pltpu.make_async_copy(source, target, load_sem.at[4 + i])
        for i, (source, target) in enumerate(
            [(b_decode, floor), (ids.at[:, rows], own_ids), (wts.at[:, rows], own_wts)]
        )
    ]
    mix_load = pltpu.make_async_copy(w_trans, mix, load_sem.at[7])
    mix_load.start()
    state_load(0).start()
    for load in smalls:
        load.start()
    for p in range(1, count):
        state_load(p).start()
    for load in later:
        load.start()
    for t in range(tiles):
        decoder_load(t).start()

    barrier = pltpu.get_barrier_semaphore()
    across = [(grp, lax.rem(doc + j, docs), voc) for j in range(1, docs)]
    along = [(grp, doc, lax.rem(voc + j, vocs)) for j in range(1, vocs)]
    for peer in across + along:
        pl.semaphore_signal(barrier, inc=1, device_id=peer, device_id_type=mesh_ids)
    for load in smalls:
        load.wait()
    mix_load.wait()

    for p in range(count):
        state_load(p).wait()
        rows = pl.ds(p * length, length)
        pre = jnp.dot(states[rows, :], mix[...], preferred_element_type=jnp.float32)
        pre = pre + shift[...][None]
        twice = pre * (1.0 + lax.erf(pre * (0.5 ** 0.5)))
        centre = twice - jnp.mean(twice, -1, keepdims=True)
        spread = jnp.mean(centre * centre, -1, keepdims=True)
        normed = centre * lax.rsqrt(spread + 4.0 * eps) * scale[...][None] + offset[...][None]
        inside = lax.broadcasted_iota(jnp.int32, (length, features), 0) < live[p]
        kept[rows, :] = jnp.where(inside, normed, normed[0:1]).astype(jnp.bfloat16)

    for load in later:
        load.wait()
    local = own_ids[...] - voc * width
    lead = jnp.clip(local >> 8, -1, leads)
    spread_to = (
        lax.broadcasted_iota(jnp.int32, (slots_per, radix), 1) % slots_per
        == lax.broadcasted_iota(jnp.int32, (slots_per, radix), 0)
    ).astype(jnp.float32).astype(jnp.bfloat16)

    def widen(value):
        value = value.astype(jnp.float32).astype(jnp.bfloat16)
        return lax.dot_general(
            value, spread_to, (((0,), (0,)), ((), ())), preferred_element_type=jnp.float32
        )

    own = (
        lax.broadcasted_iota(jnp.int32, (queries, radix), 0) % per
        == lax.broadcasted_iota(jnp.int32, (queries, radix), 1) // slots_per
    )
    hi_at[...] = jnp.where(own, widen(lead), -1.0)
    lo_at[...] = jnp.where(own, widen(local & (radix - 1)), 0.0)
    weight_at[...] = widen(own_wts[...])

    spans = leads + leads % 2
    both = 2 * per

    def made_of(at):
        high, weight = hi_at[at, :], weight_at[at, :]
        low = jnp.sum(lo_at[at, :], 0, keepdims=True)
        left = jnp.concatenate(
            [jnp.where(high == float(i), weight, 0.0) for i in range(spans)], 0
        ).astype(jnp.bfloat16)
        digits = lax.broadcasted_iota(jnp.int32, (radix, radix), 0).astype(jnp.float32)
        right = jnp.where(digits == low, 1.0, 0.0).astype(jnp.bfloat16)
        return lax.dot_general(
            left, right, (((1,), (1,)), ((), ())), preferred_element_type=jnp.float32
        )

    def build(g):
        pair = [
            made_of(pl.ds(pl.multiple_of(g * both + i * per, per), per)) for i in range(2)
        ]
        at = pl.ds(pl.multiple_of(g * both, both), both)
        for i in range(leads):
            whole = jnp.concatenate([made[i * per:(i + 1) * per] for made in pair], 0)
            top = whole.astype(jnp.bfloat16)
            big[at, i * radix:(i + 1) * radix] = top
            small[at, i * radix:(i + 1) * radix] = (
                whole - top.astype(jnp.float32)
            ).astype(jnp.bfloat16)

    def share_copy(j, step, start, cut):
        mine = slots.at[doc, :, pl.ds(start, cut)]
        return pltpu.make_async_remote_copy(
            src_ref=mine, dst_ref=mine, send_sem=doc_send.at[j, step],
            recv_sem=doc_recv.at[j, step], device_id=across[j], device_id_type=mesh_ids
        )

    def decode(t, start, begin, cut, step):
        tops = []
        for p in range(count):
            logits = jnp.dot(
                kept[p * length:(p + 1) * length, :], decoder[t, :, begin:begin + cut],
                preferred_element_type=jnp.float32
            )
            tops.append(jnp.max(logits, 0, keepdims=True))
        tops.append(jnp.zeros((pad - count, cut), jnp.float32))
        best = jnp.concatenate(tops, 0) + floor[pl.ds(start, cut)][None]
        slots[doc, :, pl.ds(start, cut)] = jnp.log1p(jnp.maximum(best, 0.0))
        for j in range(len(across)):
            share_copy(j, step, start, cut).start()

    pl.semaphore_wait(barrier, len(across) + len(along))
    rounds = queries // both
    steady = tiles - 1
    inner = rounds // max(steady, 1)

    def decode_tile(t, _):
        decoder_load(t).wait()
        for i in range(inner):
            build(t * inner + i)
        decode(t, pl.multiple_of(t * tile, tile), 0, tile, t)
        return 0

    lax.fori_loop(0, steady, decode_tile, 0)
    for g in range(inner * steady, rounds):
        build(g)
    decoder_load(steady).wait()
    cuts, begin = [], 0
    for i, cut in enumerate(pieces_of(tile)):
        start = steady * tile + begin
        decode(steady, start, begin, cut, steady + i)
        cuts.append((steady + i, start, cut))
        begin += cut

    def contract(total, step, start, cut):
        for j in range(len(across)):
            share_copy(j, step, start, cut).wait()
        value = slots[:, :, pl.ds(start, cut)].reshape(docs * pad, cut)
        top = value.astype(jnp.bfloat16)
        rest = (value - top.astype(jnp.float32)).astype(jnp.bfloat16)
        pair = jnp.concatenate([top, rest], 0)
        for table in (big, small):
            total = total + lax.dot_general(
                pair, table[:, pl.ds(start, cut)], (((1,), (1,)), ((), ())),
                preferred_element_type=jnp.float32
            )
        return total

    total = jnp.zeros((2 * docs * pad, queries), jnp.float32)
    for t in range(steady):
        total = contract(total, t, t * tile, tile)
    for step, start, cut in cuts:
        total = contract(total, step, start, cut)
    total = (total[:docs * pad] + total[docs * pad:]) * score_scale
    part[...] = total.reshape(docs, pad, queries)

    share = docs // vocs
    copies = []
    for j, peer in enumerate(along):
        copy = pltpu.make_async_remote_copy(
            src_ref=part.at[pl.ds(peer[2] * share, share)], dst_ref=parts.at[j],
            send_sem=voc_send.at[j], recv_sem=voc_recv.at[j], device_id=peer,
            device_id_type=mesh_ids
        )
        copy.start()
        copies.append(copy)
    result = part[pl.ds(voc * share, share)]
    for j, copy in enumerate(copies):
        copy.wait()
        result = result + parts[j]
    for i in range(share):
        out[i * count:(i + 1) * count, :] = result[i, :count]


def shards(
    hidden, lengths, w_trans, b_trans, ln_gain, ln_bias, w_decode, b_decode, query_ids, query_wts
):
    docs, vocs = lax.axis_size("doc"), lax.axis_size("voc")
    count, length, features = hidden.shape
    width = w_decode.shape[1]
    tile = tile_of(width)
    tiles = width // tile
    steps = tiles - 1 + len(pieces_of(tile))
    terms = query_ids.shape[1]
    queries = query_ids.shape[0] // docs
    anywhere = pl.BlockSpec(memory_space=pl.ANY)
    inside = pl.BlockSpec(memory_space=pltpu.VMEM)
    lanes = pltpu.VMEM((queries, radix), jnp.float32)
    half = pltpu.VMEM((queries, width), jnp.bfloat16)
    row = pltpu.VMEM((features,), jnp.float32)
    queue = pltpu.SemaphoreType.DMA
    return pl.pallas_call(
        functools.partial(encode_kernel, (docs, vocs), count, tile),
        out_shape=jax.ShapeDtypeStruct((docs * count // vocs, queries), jnp.float32),
        in_specs=[anywhere] * 10,
        out_specs=inside,
        scratch_shapes=[
            pltpu.VMEM((count * length, features), jnp.bfloat16),
            pltpu.VMEM((features, features), jnp.bfloat16),
            pltpu.VMEM((tiles, features, tile), jnp.bfloat16),
            pltpu.VMEM((count * length, features), jnp.bfloat16),
            pltpu.VMEM((docs, pad, width), jnp.float32),
            pltpu.VMEM((terms, queries), jnp.int32),
            pltpu.VMEM((terms, queries), jnp.int32),
            lanes, lanes, lanes,
            half, half,
            pltpu.VMEM((docs, pad, queries), jnp.float32),
            pltpu.VMEM((vocs - 1, docs // vocs, pad, queries), jnp.float32),
            pltpu.SMEM((count,), jnp.int32),
            row, row, row,
            pltpu.VMEM((width,), jnp.float32),
            queue((8,)), queue((count,)), queue((tiles,)),
            queue((docs - 1, steps)), queue((docs - 1, steps)),
            queue((vocs - 1,)), queue((vocs - 1,)),
        ],
        compiler_params=pltpu.CompilerParams(
            collective_id=0, has_side_effects=True, vmem_limit_bytes=60 * 1024 * 1024
        ),
    )(
        lengths, b_trans, ln_gain, ln_bias, b_decode,
        hidden.reshape(count * length, features), w_trans, w_decode, query_ids.T, query_wts.T
    )


def solution(mesh):
    return jax.shard_map(
        shards,
        mesh=mesh,
        in_specs=(
            P(("grp", "doc"), None, None),
            P(("grp", "doc")),
            P(),
            P(),
            P(),
            P(),
            P(None, "voc"),
            P("voc"),
            P("grp", None),
            P("grp", None),
        ),
        out_specs=P(("grp", "voc"), "doc"),
        check_vma=False,
    )
```

time: 44.7 us -> 44.5 us (level)
  no operation moved by 1% of the time
where the time goes in v1:
time: 44.5 us; the launch traced here: 44.3 us
  Pallas kernels  43 us (97%)
  local copies, waits for them, and re-layouts  1.3 us (3%)
    pallas_call x1, Pallas kernels, shards(): pl.pallas_call(functools.partial(encode_kernel, (docs, vocs), count, tile...  43 us
    unnamed x1, local copies, waits for them, and re-layouts  1.3 us

profile of v1, /device:TPU:0, one launch (start us, length us, event | category | flops | bytes accessed | tf_op | source)
XLA Modules:
  0.0 44.3 jit_solution(12782255851126639259)
XLA Ops:
  0.0 43.0 %shard_map.100 = f32[6,256]{1,0:T(8,128)} custom-call(s32[6]{0:T(128)} %lens.1, f32[768]{0:T(1024)} %b_trans.1, f32[768]{0:T(1024)} %gain.1, f32[768]{0:T(1024)} %bias.1, f32[7680]{0:T(1024)} %b_decode.1, bf16[1536,768]{1,0:T(8,128)(2,1)} %bitcast.3, bf16[768,768]{1,0:T(8,128)(2,1)} %w_trans.1, bf16[768,7680]{1,0:T(8,128)(2,1)} %w_decode.1, ...), custom_call_target="tpu_custom_call" | custom-call | tf_op jit(solution)/shard_map/pallas_call | solution.py:253
  43.0 1.3 %copy.12 = f32[6,256]{1,0:T(8,128)} copy(f32[6,256]{1,0:T(8,128)} %shard_map.100) | data formatting | bytes 12288

commit v2 on v1

--- a/solution.py
+++ b/solution.py
@@ -74,13 +74,21 @@
         state_load(p).start()
     for load in later:
         load.start()
-    for t in range(tiles):
-        decoder_load(t).start()
-
     barrier = pltpu.get_barrier_semaphore()
-    across = [(grp, lax.rem(doc + j, docs), voc) for j in range(1, docs)]
+    cores = 2 - docs % 2
+    chips = docs // cores
+    chip, core = doc // cores, lax.rem(doc, cores)
+    beside = cores - 1 - core
+
+    def mate(shift, side):
+        return cores * lax.rem(chip + shift, chips) + side
+
+    links = [(mate(h, core), mate(chips - h, core)) for h in range(1, chips)]
+    direct = len(links)
+    if cores == 2:
+        links += [(mate(h, beside), mate(chips - h, beside)) for h in range(chips)]
     along = [(grp, doc, lax.rem(voc + j, vocs)) for j in range(1, vocs)]
-    for peer in across + along:
+    for peer in [(grp, target, voc) for target, _ in links] + along:
         pl.semaphore_signal(barrier, inc=1, device_id=peer, device_id_type=mesh_ids)
     for load in smalls:
         load.wait()
@@ -88,6 +96,8 @@
 
     for p in range(count):
         state_load(p).wait()
+        for t in range(p * tiles // count, (p + 1) * tiles // count):
+            decoder_load(t).start()
         rows = pl.ds(p * length, length)
         pre = jnp.dot(states[rows, :], mix[...], preferred_element_type=jnp.float32)
         pre = pre + shift[...][None]
@@ -149,14 +159,23 @@
                 whole - top.astype(jnp.float32)
             ).astype(jnp.bfloat16)
 
-    def share_copy(j, step, start, cut):
-        mine = slots.at[doc, :, pl.ds(start, cut)]
+    def share_copy(j, step, start, cut, passed=False):
+        target, source = links[j]
+        if passed:
+            target, source = mate(0, beside), links[j - direct - 1][1]
+        mine = slots.at[source if passed else doc, :, pl.ds(start, cut)]
         return pltpu.make_async_remote_copy(
             src_ref=mine, dst_ref=mine, send_sem=doc_send.at[j, step],
-            recv_sem=doc_recv.at[j, step], device_id=across[j], device_id_type=mesh_ids
-        )
-
-    def decode(t, start, begin, cut, step):
+            recv_sem=doc_recv.at[j, step], device_id=(grp, target, voc),
+            device_id_type=mesh_ids
+        )
+
+    def hand_on(step, start, cut):
+        for j in range(direct + 1, len(links)):
+            share_copy(j - direct - 1, step, start, cut).wait_recv()
+            share_copy(j, step, start, cut, True).start()
+
+    def decode(t, start, begin, cut, step, whole=False):
         tops = []
         for p in range(count):
             logits = jnp.dot(
@@ -167,10 +186,9 @@
         tops.append(jnp.zeros((pad - count, cut), jnp.float32))
         best = jnp.concatenate(tops, 0) + floor[pl.ds(start, cut)][None]
         slots[doc, :, pl.ds(start, cut)] = jnp.log1p(jnp.maximum(best, 0.0))
-        for j in range(len(across)):
+        for j in range(len(links) if whole else min(direct + 1, len(links))):
             share_copy(j, step, start, cut).start()
 
-    pl.semaphore_wait(barrier, len(across) + len(along))
     rounds = queries // both
     steady = tiles - 1
     inner = rounds // max(steady, 1)
@@ -179,7 +197,18 @@
         decoder_load(t).wait()
         for i in range(inner):
             build(t * inner + i)
-        decode(t, pl.multiple_of(t * tile, tile), 0, tile, t)
+
+        @pl.when(t == 0)
+        def _():
+            pl.semaphore_wait(barrier, len(links) + len(along))
+
+        start = pl.multiple_of(t * tile, tile)
+        decode(t, start, 0, tile, t)
+
+        @pl.when(t > 0)
+        def _():
+            hand_on(t - 1, pl.multiple_of(start - tile, tile), tile)
+
         return 0
 
     lax.fori_loop(0, steady, decode_tile, 0)
@@ -189,13 +218,20 @@
     cuts, begin = [], 0
     for i, cut in enumerate(pieces_of(tile)):
         start = steady * tile + begin
-        decode(steady, start, begin, cut, steady + i)
-        cuts.append((steady + i, start, cut))
+        whole = i > 0
+        decode(steady, start, begin, cut, steady + i, whole)
+        if i == 0:
+            hand_on(steady - 1, start - tile, tile)
+        cuts.append((steady + i, start, cut, not whole))
         begin += cut
 
-    def contract(total, step, start, cut):
-        for j in range(len(across)):
-            share_copy(j, step, start, cut).wait()
+    def contract(total, step, start, cut, passed):
+        for j in range(len(links)):
+            relay = passed and j > direct
+            copy = share_copy(j, step, start, cut, relay)
+            copy.wait_send()
+            if not (passed and j < direct):
+                copy.wait_recv()
         value = slots[:, :, pl.ds(start, cut)].reshape(docs * pad, cut)
         top = value.astype(jnp.bfloat16)
         rest = (value - top.astype(jnp.float32)).astype(jnp.bfloat16)
@@ -209,9 +245,11 @@
 
     total = jnp.zeros((2 * docs * pad, queries), jnp.float32)
     for t in range(steady):
-        total = contract(total, t, t * tile, tile)
-    for step, start, cut in cuts:
-        total = contract(total, step, start, cut)
+        total = contract(total, t, t * tile, tile, True)
+        if t == 0:
+            hand_on(*cuts[0][:3])
+    for cut in cuts:
+        total = contract(total, *cut)
     total = (total[:docs * pad] + total[docs * pad:]) * score_scale
     part[...] = total.reshape(docs, pad, queries)
 

time: 44.5 us -> 44.6 us (level)
  no operation moved by 1% of the time
where the time goes in v2:
time: 44.6 us; the launch traced here: 44.4 us
  Pallas kernels  43.1 us (97%)
  local copies, waits for them, and re-layouts  1.3 us (3%)
    pallas_call x1, Pallas kernels, shards(): pl.pallas_call(functools.partial(encode_kernel, (docs, vocs), count, tile...  43.1 us
    unnamed x1, local copies, waits for them, and re-layouts  1.3 us

profile of v2, /device:TPU:0, one launch (start us, length us, event | category | flops | bytes accessed | tf_op | source)
XLA Modules:
  0.0 44.4 jit_solution(9504793040329355358)
XLA Ops:
  0.0 43.1 %shard_map.100 = f32[6,256]{1,0:T(8,128)} custom-call(s32[6]{0:T(128)} %lens.1, f32[768]{0:T(1024)} %b_trans.1, f32[768]{0:T(1024)} %gain.1, f32[768]{0:T(1024)} %bias.1, f32[7680]{0:T(1024)} %b_decode.1, bf16[1536,768]{1,0:T(8,128)(2,1)} %bitcast.3, bf16[768,768]{1,0:T(8,128)(2,1)} %w_trans.1, bf16[768,7680]{1,0:T(8,128)(2,1)} %w_decode.1, ...), custom_call_target="tpu_custom_call" | custom-call | tf_op jit(solution)/shard_map/pallas_call | solution.py:291
  43.1 1.3 %copy.12 = f32[6,256]{1,0:T(8,128)} copy(f32[6,256]{1,0:T(8,128)} %shard_map.100) | data formatting | bytes 12288

commit v3 on v1

v3 whole, which is shorter than its diff:
```python
import functools

import jax
import jax.numpy as jnp
from jax import lax
from jax.experimental import pallas as pl
from jax.experimental.pallas import tpu as pltpu
from jax.sharding import PartitionSpec as P

eps = 1e-06
score_scale = 1.0 / 1024.0
radix = 256
pad = 8


def tile_of(width):
    best = 128
    for tile in range(128, 1537, 128):
        if width % tile == 0:
            best = tile
    return best


def pieces_of(tile):
    if tile < 768 or tile % 256:
        return [tile]
    first = tile // 512 * 256
    return [cut for cut in (first, tile - first - 256, 256) if cut]


def encode_kernel(
    sizes, count, tile, lens, b_trans, gain, bias, b_decode, hidden, w_trans, w_decode, ids, wts,
    out, states, mix, decoder, kept, slots, own_ids, own_wts, hi_at, lo_at, weight_at, big, small,
    part, parts, live, shift, scale, offset, floor,
    load_sem, state_sem, decoder_sem, doc_send, doc_recv, voc_send, voc_recv
):
    docs, vocs = sizes
    length, features = hidden.shape[0] // count, hidden.shape[1]
    width = w_decode.shape[1]
    tiles = width // tile
    slots_per, queries = own_ids.shape
    per = radix // slots_per
    leads = width // radix
    grp, doc, voc = (lax.axis_index(name) for name in ("grp", "doc", "voc"))
    mesh_ids = pl.DeviceIdType.MESH

    def state_load(p):
        rows = pl.ds(p * length, length)
        return pltpu.make_async_copy(hidden.at[rows], states.at[rows], state_sem.at[p])

    def decoder_load(t):
        cut = pl.ds(pl.multiple_of(t * tile, tile), tile)
        return pltpu.make_async_copy(w_decode.at[:, cut], decoder.at[t], decoder_sem.at[t])

    rows = pl.ds(pl.multiple_of(doc * queries, queries), queries)
    loads = [
        pltpu.make_async_copy(source, target, load_sem.at[i])
        for i, (source, target) in enumerate([
            (ids.at[:, rows], own_ids), (wts.at[:, rows], own_wts), (w_trans, mix),
            (lens, live), (b_trans, shift), (gain, scale), (bias, offset), (b_decode, floor),
        ])
    ]
    for load in loads[:3]:
        load.start()
    state_load(0).start()
    for load in loads[3:]:
        load.start()
    for p in range(1, count):
        state_load(p).start()

    cores = 2 - docs % 2
    chips = docs // cores
    chip, core = doc // cores, lax.rem(doc, cores)

    def mate(shift, side):
        return cores * lax.rem(chip + shift, chips) + side

    links = [
        [
            (mate(h, side), mate(chips - h, side))
            for side in ([core, cores - 1 - core] if cores == 2 else [core])
            if h or side is not core
        ]
        for h in range(chips)
    ]
    first_link = [sum(len(links[k]) for k in range(h)) for h in range(chips)]
    barrier = pltpu.get_barrier_semaphore()
    peers = [(grp, target, voc) for group in links for target, _ in group]
    along = [(grp, doc, lax.rem(voc + j, vocs)) for j in range(1, vocs)]
    for peer in peers + along:
        pl.semaphore_signal(barrier, inc=1, device_id=peer, device_id_type=mesh_ids)

    for load in loads[:2]:
        load.wait()
    local = own_ids[...] - voc * width
    lead = jnp.clip(local >> 8, -1, leads)
    spread_to = (
        lax.broadcasted_iota(jnp.int32, (slots_per, radix), 1) % slots_per
        == lax.broadcasted_iota(jnp.int32, (slots_per, radix), 0)
    ).astype(jnp.float32).astype(jnp.bfloat16)

    def widen(value):
        value = value.astype(jnp.float32).astype(jnp.bfloat16)
        return lax.dot_general(
            value, spread_to, (((0,), (0,)), ((), ())), preferred_element_type=jnp.float32
        )

    own = (
        lax.broadcasted_iota(jnp.int32, (queries, radix), 0) % per
        == lax.broadcasted_iota(jnp.int32, (queries, radix), 1) // slots_per
    )
    hi_at[...] = jnp.where(own, widen(lead), -1.0)
    lo_at[...] = jnp.where(own, widen(local & (radix - 1)), 0.0)
    weight_at[...] = widen(own_wts[...])
    for load in loads[2:]:
        load.wait()

    for p in range(count):
        state_load(p).wait()
        for t in range(p * tiles // count, (p + 1) * tiles // count):
            decoder_load(t).start()
        rows = pl.ds(p * length, length)
        pre = jnp.dot(states[rows, :], mix[...], preferred_element_type=jnp.float32)
        pre = pre + shift[...][None]
        twice = pre * (1.0 + lax.erf(pre * (0.5 ** 0.5)))
        centre = twice - jnp.mean(twice, -1, keepdims=True)
        spread = jnp.mean(centre * centre, -1, keepdims=True)
        normed = centre * lax.rsqrt(spread + 4.0 * eps) * scale[...][None] + offset[...][None]
        inside = lax.broadcasted_iota(jnp.int32, (length, features), 0) < live[p]
        kept[rows, :] = jnp.where(inside, normed, normed[0:1]).astype(jnp.bfloat16)

    spans = leads + leads % 2
    both = 2 * per

    def made_of(first):
        at = pl.ds(first, per)
        high, weight = hi_at[at, :], weight_at[at, :]
        low = jnp.sum(lo_at[at, :], 0, keepdims=True)
        left = jnp.concatenate(
            [jnp.where(high == float(i), weight, 0.0) for i in range(spans)], 0
        ).astype(jnp.bfloat16)
        digits = lax.broadcasted_iota(jnp.int32, (radix, radix), 0).astype(jnp.float32)
        right = jnp.where(digits == low, 1.0, 0.0).astype(jnp.bfloat16)
        return lax.dot_general(
            left, right, (((1,), (1,)), ((), ())), preferred_element_type=jnp.float32
        )

    def build(g):
        pair = [made_of(g * both + i * per) for i in range(2)]
        at = pl.ds(g * both, both)
        for i in range(leads):
            whole = jnp.concatenate([made[i * per:(i + 1) * per] for made in pair], 0)
            top = whole.astype(jnp.bfloat16)
            big[at, i * radix:(i + 1) * radix] = top
            small[at, i * radix:(i + 1) * radix] = (
                whole - top.astype(jnp.float32)
            ).astype(jnp.bfloat16)

    def share_copy(j, target, cut):
        step, start, size = cut
        mine = slots.at[doc, :, pl.ds(start, size)]
        return pltpu.make_async_remote_copy(
            src_ref=mine, dst_ref=mine, send_sem=doc_send.at[j, step],
            recv_sem=doc_recv.at[j, step], device_id=(grp, target, voc),
            device_id_type=mesh_ids
        )

    def arrive(h, cut):
        for j, (target, _) in enumerate(links[h]):
            share_copy(first_link[h] + j, target, cut).wait()

    def decode(t, begin, cut, between):
        step, start, size = cut
        tops = []
        for p in range(count):
            logits = jnp.dot(
                kept[p * length:(p + 1) * length, :], decoder[t, :, begin:begin + size],
                preferred_element_type=jnp.float32
            )
            tops.append(jnp.max(logits, 0, keepdims=True))
            if p == count // 2 and between is not None:
                between()
        tops.append(jnp.zeros((pad - count, size), jnp.float32))
        best = jnp.concatenate(tops, 0) + floor[pl.ds(start, size)][None]
        slots[doc, :, pl.ds(start, size)] = jnp.log1p(jnp.maximum(best, 0.0))
        for h in reversed(range(chips)):
            for j, (target, _) in enumerate(links[h]):
                share_copy(first_link[h] + j, target, cut).start()

    def contract(docs_at, many, cuts):
        total = jnp.zeros((2 * many * pad, queries), jnp.float32)
        for _, start, size in cuts:
            value = slots[docs_at, :, pl.ds(start, size)].reshape(many * pad, size)
            top = value.astype(jnp.bfloat16)
            rest = (value - top.astype(jnp.float32)).astype(jnp.bfloat16)
            pair = jnp.concatenate([top, rest], 0)
            for table in (big, small):
                total = total + lax.dot_general(
                    pair, table[:, pl.ds(start, size)], (((1,), (1,)), ((), ())),
                    preferred_element_type=jnp.float32
                )
        total = (total[:many * pad] + total[many * pad:]) * score_scale
        return total.reshape(many, pad, queries)

    rounds = queries // both
    early = max(1, min(2, tiles - 1))
    whole_tiles = [(t, t * tile, tile) for t in range(tiles - 1)]
    pieces, begin = [], (tiles - 1) * tile
    for size in pieces_of(tile):
        pieces.append((len(whole_tiles) + len(pieces), begin, size))
        begin += size
    part[...] = jnp.zeros_like(part)

    def add_all(cut):
        for h in range(chips):
            arrive(h, cut)
        part[...] += contract(pl.ds(0, docs), docs, [cut])

    ready = 0
    for t in range(tiles):
        decoder_load(t).wait()
        for g in range(rounds * t // early, rounds * (t + 1) // early):
            if t < early:
                build(g)
        if t == 0:
            pl.semaphore_wait(barrier, len(peers) + len(along))
        for i, cut in enumerate(whole_tiles[t:t + 1] or pieces):
            between = None
            if t >= 2 and t >= early and i == 0:
                between = functools.partial(add_all, whole_tiles[ready])
                ready += 1
            decode(t, cut[1] - t * tile, cut, between)

    share = docs // vocs
    for h in range(chips):
        for cut in whole_tiles[ready:] + pieces:
            arrive(h, cut)
        at = cores * lax.rem(chip + chips - h, chips)
        part[pl.ds(at, cores)] += contract(
            pl.ds(at, cores), cores, whole_tiles[ready:] + pieces
        )
        for i in range(cores):
            item = at + i
            goal = item // share
            hop = lax.rem(goal + vocs - voc, vocs)

            @pl.when(hop != 0)
            def _():
                pltpu.make_async_remote_copy(
                    src_ref=part.at[item], dst_ref=parts.at[hop - 1, lax.rem(item, share)],
                    send_sem=voc_send.at[hop - 1, lax.rem(item, share)],
                    recv_sem=voc_recv.at[hop - 1, lax.rem(item, share)],
                    device_id=(grp, doc, goal), device_id_type=mesh_ids
                ).start()

    result = part[pl.ds(voc * share, share)]
    for j, peer in enumerate(along):
        for i in range(share):
            pltpu.make_async_remote_copy(
                src_ref=part.at[peer[2] * share + i], dst_ref=parts.at[j, i],
                send_sem=voc_send.at[j, i], recv_sem=voc_recv.at[j, i], device_id=peer,
                device_id_type=mesh_ids
            ).wait()
        result = result + parts[j]
    for i in range(share):
        out[i * count:(i + 1) * count, :] = result[i, :count]


def shards(
    hidden, lengths, w_trans, b_trans, ln_gain, ln_bias, w_decode, b_decode, query_ids, query_wts
):
    docs, vocs = lax.axis_size("doc"), lax.axis_size("voc")
    count, length, features = hidden.shape
    width = w_decode.shape[1]
    tile = tile_of(width)
    tiles = width // tile
    steps = tiles - 1 + len(pieces_of(tile))
    terms = query_ids.shape[1]
    queries = query_ids.shape[0] // docs
    anywhere = pl.BlockSpec(memory_space=pl.ANY)
    inside = pl.BlockSpec(memory_space=pltpu.VMEM)
    lanes = pltpu.VMEM((queries, radix), jnp.float32)
    half = pltpu.VMEM((queries, width), jnp.bfloat16)
    row = pltpu.VMEM((features,), jnp.float32)
    queue = pltpu.SemaphoreType.DMA
    return pl.pallas_call(
        functools.partial(encode_kernel, (docs, vocs), count, tile),
        out_shape=jax.ShapeDtypeStruct((docs * count // vocs, queries), jnp.float32),
        in_specs=[anywhere] * 10,
        out_specs=inside,
        scratch_shapes=[
            pltpu.VMEM((count * length, features), jnp.bfloat16),
            pltpu.VMEM((features, features), jnp.bfloat16),
            pltpu.VMEM((tiles, features, tile), jnp.bfloat16),
            pltpu.VMEM((count * length, features), jnp.bfloat16),
            pltpu.VMEM((docs, pad, width), jnp.float32),
            pltpu.VMEM((terms, queries), jnp.int32),
            pltpu.VMEM((terms, queries), jnp.int32),
            lanes, lanes, lanes,
            half, half,
            pltpu.VMEM((docs, pad, queries), jnp.float32),
            pltpu.VMEM((vocs - 1, docs // vocs, pad, queries), jnp.float32),
            pltpu.SMEM((count,), jnp.int32),
            row, row, row,
            pltpu.VMEM((width,), jnp.float32),
            queue((8,)), queue((count,)), queue((tiles,)),
            queue((docs - 1, steps)), queue((docs - 1, steps)),
            queue((vocs - 1, docs // vocs)), queue((vocs - 1, docs // vocs)),
        ],
        compiler_params=pltpu.CompilerParams(
            collective_id=0, has_side_effects=True, vmem_limit_bytes=60 * 1024 * 1024
        ),
    )(
        lengths, b_trans, ln_gain, ln_bias, b_decode,
        hidden.reshape(count * length, features), w_trans, w_decode, query_ids.T, query_wts.T
    )


def solution(mesh):
    return jax.shard_map(
        shards,
        mesh=mesh,
        in_specs=(
            P(("grp", "doc"), None, None),
            P(("grp", "doc")),
            P(),
            P(),
            P(),
            P(),
            P(None, "voc"),
            P("voc"),
            P("grp", None),
            P("grp", None),
        ),
        out_specs=P(("grp", "voc"), "doc"),
        check_vma=False,
    )
```

time: 44.5 us -> 42.4 us (0.953)
  the two profiles are of different devices: /device:TPU:0 before, /device:TPU:2 now
where the time goes in v3:
time: 42.4 us; the launch traced here: 42.2 us
  Pallas kernels  40.8 us (96%)
  local copies, waits for them, and re-layouts  1.3 us (3%)
    pallas_call x1, Pallas kernels, shards(): pl.pallas_call(functools.partial(encode_kernel, (docs, vocs), count, tile...  40.8 us
    unnamed x1, local copies, waits for them, and re-layouts  1.3 us

profile of v3, /device:TPU:2, one launch (start us, length us, event | category | flops | bytes accessed | tf_op | source)
XLA Modules:
  0.0 42.2 jit_solution(9232054174313635425)
XLA Ops:
  0.0 40.8 %shard_map.100 = f32[6,256]{1,0:T(8,128)} custom-call(s32[6]{0:T(128)} %lens.1, f32[768]{0:T(1024)} %b_trans.1, f32[768]{0:T(1024)} %gain.1, f32[768]{0:T(1024)} %bias.1, f32[7680]{0:T(1024)} %b_decode.1, bf16[1536,768]{1,0:T(8,128)(2,1)} %bitcast.3, bf16[768,768]{1,0:T(8,128)(2,1)} %w_trans.1, bf16[768,7680]{1,0:T(8,128)(2,1)} %w_decode.1, ...), custom_call_target="tpu_custom_call" | custom-call | tf_op jit(solution)/shard_map/pallas_call | solution.py:286
  40.9 1.3 %copy.12 = f32[6,256]{1,0:T(8,128)} copy(f32[6,256]{1,0:T(8,128)} %shard_map.100) | data formatting | bytes 12288

commit v4 on v3

--- a/solution.py
+++ b/solution.py
@@ -116,8 +116,9 @@
         load.wait()
 
     for p in range(count):
-        state_load(p).wait()
-        for t in range(p * tiles // count, (p + 1) * tiles // count):
+        for later in {0: range(min(2, count)), 2: range(2, count)}.get(p, ()):
+            state_load(later).wait()
+        for t in {0: range(min(2, tiles)), 2: range(2, tiles)}.get(p, ()):
             decoder_load(t).start()
         rows = pl.ds(p * length, length)
         pre = jnp.dot(states[rows, :], mix[...], preferred_element_type=jnp.float32)
@@ -216,7 +217,17 @@
             arrive(h, cut)
         part[...] += contract(pl.ds(0, docs), docs, [cut])
 
-    ready = 0
+    def first_doc(h):
+        return cores * lax.rem(chip + chips - h, chips)
+
+    def add(h, cuts):
+        for cut in cuts:
+            arrive(h, cut)
+        at = pl.ds(first_doc(h), cores)
+        part[at] += contract(at, cores, cuts)
+
+    ready = max(0, tiles - max(2, early))
+    remain = whole_tiles[ready:]
     for t in range(tiles):
         decoder_load(t).wait()
         for g in range(rounds * t // early, rounds * (t + 1) // early):
@@ -226,21 +237,17 @@
             pl.semaphore_wait(barrier, len(peers) + len(along))
         for i, cut in enumerate(whole_tiles[t:t + 1] or pieces):
             between = None
-            if t >= 2 and t >= early and i == 0:
-                between = functools.partial(add_all, whole_tiles[ready])
-                ready += 1
+            if t >= max(2, early) and i == 0:
+                between = functools.partial(add_all, whole_tiles[t - max(2, early)])
+            if t == tiles - 1 and i == 1:
+                between = functools.partial(add, 0, remain)
             decode(t, cut[1] - t * tile, cut, between)
 
     share = docs // vocs
-    for h in range(chips):
-        for cut in whole_tiles[ready:] + pieces:
-            arrive(h, cut)
-        at = cores * lax.rem(chip + chips - h, chips)
-        part[pl.ds(at, cores)] += contract(
-            pl.ds(at, cores), cores, whole_tiles[ready:] + pieces
-        )
+
+    def give_out(h):
         for i in range(cores):
-            item = at + i
+            item = first_doc(h) + i
             goal = item // share
             hop = lax.rem(goal + vocs - voc, vocs)
 
@@ -252,6 +259,20 @@
                     recv_sem=voc_recv.at[hop - 1, lax.rem(item, share)],
                     device_id=(grp, doc, goal), device_id_type=mesh_ids
                 ).start()
+
+    if len(pieces) == 1:
+        add(0, remain)
+    if len(pieces) > 1:
+        add(0, pieces[:-1])
+    for h in range(1, chips):
+        add(h, remain)
+    add(0, pieces[-1:])
+    give_out(0)
+    for h in range(1, chips):
+        if len(pieces) > 1:
+            add(h, pieces[:-1])
+        add(h, pieces[-1:])
+        give_out(h)
 
     result = part[pl.ds(voc * share, share)]
     for j, peer in enumerate(along):

time: 42.4 us -> 40.6 us (0.958)
  Pallas kernels: 40.8 us -> 38.7 us
    pallas_call x1, Pallas kernels: 40.8 us -> 38.7 us  [shards(): pl.pallas_call(functools.partial(encode_kernel, (docs, vocs), count, tile...]
where the time goes in v4:
time: 40.6 us; the launch traced here: 40 us
  Pallas kernels  38.7 us (95%)
  local copies, waits for them, and re-layouts  1.3 us (3%)
    pallas_call x1, Pallas kernels, shards(): pl.pallas_call(functools.partial(encode_kernel, (docs, vocs), count, tile...  38.7 us
    unnamed x1, local copies, waits for them, and re-layouts  1.3 us

profile of v4, /device:TPU:2, one launch (start us, length us, event | category | flops | bytes accessed | tf_op | source)
XLA Modules:
  0.0 40.0 jit_solution(5110732081298298309)
XLA Ops:
  0.0 38.7 %shard_map.100 = f32[6,256]{1,0:T(8,128)} custom-call(s32[6]{0:T(128)} %lens.1, f32[768]{0:T(1024)} %b_trans.1, f32[768]{0:T(1024)} %gain.1, f32[768]{0:T(1024)} %bias.1, f32[7680]{0:T(1024)} %b_decode.1, bf16[1536,768]{1,0:T(8,128)(2,1)} %bitcast.3, bf16[768,768]{1,0:T(8,128)(2,1)} %w_trans.1, bf16[768,7680]{1,0:T(8,128)(2,1)} %w_decode.1, ...), custom_call_target="tpu_custom_call" | custom-call | tf_op jit(solution)/shard_map/pallas_call | solution.py:307
  38.7 1.3 %copy.12 = f32[6,256]{1,0:T(8,128)} copy(f32[6,256]{1,0:T(8,128)} %shard_map.100) | data formatting | bytes 12288

commit v5 on v4

--- a/solution.py
+++ b/solution.py
@@ -220,11 +220,12 @@
     def first_doc(h):
         return cores * lax.rem(chip + chips - h, chips)
 
-    def add(h, cuts):
+    def add(first, many, cuts, h=None):
         for cut in cuts:
-            arrive(h, cut)
-        at = pl.ds(first_doc(h), cores)
-        part[at] += contract(at, cores, cuts)
+            if h is not None:
+                arrive(h, cut)
+        at = pl.ds(first, many)
+        part[at] += contract(at, many, cuts)
 
     ready = max(0, tiles - max(2, early))
     remain = whole_tiles[ready:]
@@ -240,39 +241,45 @@
             if t >= max(2, early) and i == 0:
                 between = functools.partial(add_all, whole_tiles[t - max(2, early)])
             if t == tiles - 1 and i == 1:
-                between = functools.partial(add, 0, remain)
+                between = functools.partial(add, first_doc(0), cores, remain, 0)
+            if t == tiles - 1 and i == 2:
+                between = functools.partial(add, doc, 1, pieces[:-1])
             decode(t, cut[1] - t * tile, cut, between)
 
     share = docs // vocs
 
-    def give_out(h):
-        for i in range(cores):
-            item = first_doc(h) + i
-            goal = item // share
-            hop = lax.rem(goal + vocs - voc, vocs)
-
-            @pl.when(hop != 0)
-            def _():
-                pltpu.make_async_remote_copy(
-                    src_ref=part.at[item], dst_ref=parts.at[hop - 1, lax.rem(item, share)],
-                    send_sem=voc_send.at[hop - 1, lax.rem(item, share)],
-                    recv_sem=voc_recv.at[hop - 1, lax.rem(item, share)],
-                    device_id=(grp, doc, goal), device_id_type=mesh_ids
-                ).start()
-
-    if len(pieces) == 1:
-        add(0, remain)
-    if len(pieces) > 1:
-        add(0, pieces[:-1])
+    def give_out(item):
+        goal = item // share
+        hop = lax.rem(goal + vocs - voc, vocs)
+
+        @pl.when(hop != 0)
+        def _():
+            pltpu.make_async_remote_copy(
+                src_ref=part.at[item], dst_ref=parts.at[hop - 1, lax.rem(item, share)],
+                send_sem=voc_send.at[hop - 1, lax.rem(item, share)],
+                recv_sem=voc_recv.at[hop - 1, lax.rem(item, share)],
+                device_id=(grp, doc, goal), device_id_type=mesh_ids
+            ).start()
+
+    if len(pieces) < 2:
+        add(first_doc(0), cores, remain, 0)
+    if len(pieces) == 2:
+        add(doc, 1, pieces[:-1])
+    add(doc, 1, pieces[-1:])
+    give_out(doc)
+    if cores == 2 and len(pieces) > 1:
+        add(mate(0, 1 - core), 1, pieces[:-1], 0)
     for h in range(1, chips):
-        add(h, remain)
-    add(0, pieces[-1:])
-    give_out(0)
+        add(first_doc(h), cores, remain, h)
+    if cores == 2:
+        add(mate(0, 1 - core), 1, pieces[-1:], 0)
+        give_out(mate(0, 1 - core))
     for h in range(1, chips):
         if len(pieces) > 1:
-            add(h, pieces[:-1])
-        add(h, pieces[-1:])
-        give_out(h)
+            add(first_doc(h), cores, pieces[:-1], h)
+        add(first_doc(h), cores, pieces[-1:], h)
+        for i in range(cores):
+            give_out(first_doc(h) + i)
 
     result = part[pl.ds(voc * share, share)]
     for j, peer in enumerate(along):
@@ -306,7 +313,7 @@
     queue = pltpu.SemaphoreType.DMA
     return pl.pallas_call(
         functools.partial(encode_kernel, (docs, vocs), count, tile),
-        out_shape=jax.ShapeDtypeStruct((docs * count // vocs, queries), jnp.float32),
+        out_shape=pltpu.VMEM((docs * count // vocs, queries), jnp.float32),
         in_specs=[anywhere] * 10,
         out_specs=inside,
         scratch_shapes=[

time: 40.6 us -> 39.5 us (0.973); the launches traced: 40 us -> 39.3 us
  local copies, waits for them, and re-layouts: 1.3 us -> 0.6 us
    unnamed x1, local copies, waits for them, and re-layouts: 1.3 us -> 0.6 us
where the time goes in v5:
time: 39.5 us; the launch traced here: 39.3 us
  Pallas kernels  38.7 us (98%)
  local copies, waits for them, and re-layouts  0.6 us (2%)
    pallas_call x1, Pallas kernels, shards(): pl.pallas_call(functools.partial(encode_kernel, (docs, vocs), count, tile...  38.7 us

profile of v5, /device:TPU:2, one launch (start us, length us, event | category | flops | bytes accessed | tf_op | source)
XLA Modules:
  0.0 39.3 jit_solution(14629338733724314183)
XLA Ops:
  0.0 38.7 %shard_map.100 = f32[6,256]{1,0:T(8,128)S(1)} custom-call(s32[6]{0:T(128)} %lens.1, f32[768]{0:T(1024)} %b_trans.1, f32[768]{0:T(1024)} %gain.1, f32[768]{0:T(1024)} %bias.1, f32[7680]{0:T(1024)} %b_decode.1, bf16[1536,768]{1,0:T(8,128)(2,1)} %bitcast.3, bf16[768,768]{1,0:T(8,128)(2,1)} %w_trans.1, bf16[768,7680]{1,0:T(8,128)(2,1)} %w_decode.1, ...), custom_call_target="tpu_custom_call" | custom-call | tf_op jit(solution)/shard_map/pallas_call | solution.py:314
  38.7 0.6 %copy.12 = f32[6,256]{1,0:T(8,128)} copy(f32[6,256]{1,0:T(8,128)S(1)} %shard_map.100) | data formatting | bytes 12288

commit v6 on v5

--- a/solution.py
+++ b/solution.py
@@ -112,6 +112,37 @@
     hi_at[...] = jnp.where(own, widen(lead), -1.0)
     lo_at[...] = jnp.where(own, widen(local & (radix - 1)), 0.0)
     weight_at[...] = widen(own_wts[...])
+    spans = leads + leads % 2
+    both = 2 * per
+    rounds = queries // both
+    ahead = rounds * 8 // 16
+
+    def made_of(first):
+        at = pl.ds(first, per)
+        high, weight = hi_at[at, :], weight_at[at, :]
+        low = jnp.sum(lo_at[at, :], 0, keepdims=True)
+        left = jnp.concatenate(
+            [jnp.where(high == float(i), weight, 0.0) for i in range(spans)], 0
+        ).astype(jnp.bfloat16)
+        digits = lax.broadcasted_iota(jnp.int32, (radix, radix), 0).astype(jnp.float32)
+        right = jnp.where(digits == low, 1.0, 0.0).astype(jnp.bfloat16)
+        return lax.dot_general(
+            left, right, (((1,), (1,)), ((), ())), preferred_element_type=jnp.float32
+        )
+
+    def build(g):
+        pair = [made_of(g * both + i * per) for i in range(2)]
+        at = pl.ds(g * both, both)
+        for i in range(leads):
+            whole = jnp.concatenate([made[i * per:(i + 1) * per] for made in pair], 0)
+            top = whole.astype(jnp.bfloat16)
+            big[at, i * radix:(i + 1) * radix] = top
+            small[at, i * radix:(i + 1) * radix] = (
+                whole - top.astype(jnp.float32)
+            ).astype(jnp.bfloat16)
+
+    for g in range(ahead):
+        build(g)
     for load in loads[2:]:
         load.wait()
 
@@ -129,33 +160,6 @@
         normed = centre * lax.rsqrt(spread + 4.0 * eps) * scale[...][None] + offset[...][None]
         inside = lax.broadcasted_iota(jnp.int32, (length, features), 0) < live[p]
         kept[rows, :] = jnp.where(inside, normed, normed[0:1]).astype(jnp.bfloat16)
-
-    spans = leads + leads % 2
-    both = 2 * per
-
-    def made_of(first):
-        at = pl.ds(first, per)
-        high, weight = hi_at[at, :], weight_at[at, :]
-        low = jnp.sum(lo_at[at, :], 0, keepdims=True)
-        left = jnp.concatenate(
-            [jnp.where(high == float(i), weight, 0.0) for i in range(spans)], 0
-        ).astype(jnp.bfloat16)
-        digits = lax.broadcasted_iota(jnp.int32, (radix, radix), 0).astype(jnp.float32)
-        right = jnp.where(digits == low, 1.0, 0.0).astype(jnp.bfloat16)
-        return lax.dot_general(
-            left, right, (((1,), (1,)), ((), ())), preferred_element_type=jnp.float32
-        )
-
-    def build(g):
-        pair = [made_of(g * both + i * per) for i in range(2)]
-        at = pl.ds(g * both, both)
-        for i in range(leads):
-            whole = jnp.concatenate([made[i * per:(i + 1) * per] for made in pair], 0)
-            top = whole.astype(jnp.bfloat16)
-            big[at, i * radix:(i + 1) * radix] = top
-            small[at, i * radix:(i + 1) * radix] = (
-                whole - top.astype(jnp.float32)
-            ).astype(jnp.bfloat16)
 
     def share_copy(j, target, cut):
         step, start, size = cut
@@ -203,7 +207,6 @@
         total = (total[:many * pad] + total[many * pad:]) * score_scale
         return total.reshape(many, pad, queries)
 
-    rounds = queries // both
     early = max(1, min(2, tiles - 1))
     whole_tiles = [(t, t * tile, tile) for t in range(tiles - 1)]
     pieces, begin = [], (tiles - 1) * tile
@@ -227,11 +230,17 @@
         at = pl.ds(first, many)
         part[at] += contract(at, many, cuts)
 
+    def add_before_last():
+        add(first_doc(0), cores, pieces[:1], 0)
+        add(doc, 1, pieces[1:-1])
+
     ready = max(0, tiles - max(2, early))
     remain = whole_tiles[ready:]
     for t in range(tiles):
         decoder_load(t).wait()
-        for g in range(rounds * t // early, rounds * (t + 1) // early):
+        for g in range(
+            ahead + (rounds - ahead) * t // early, ahead + (rounds - ahead) * (t + 1) // early
+        ):
             if t < early:
                 build(g)
         if t == 0:
@@ -243,7 +252,7 @@
             if t == tiles - 1 and i == 1:
                 between = functools.partial(add, first_doc(0), cores, remain, 0)
             if t == tiles - 1 and i == 2:
-                between = functools.partial(add, doc, 1, pieces[:-1])
+                between = add_before_last
             decode(t, cut[1] - t * tile, cut, between)
 
     share = docs // vocs
@@ -263,21 +272,18 @@
 
     if len(pieces) < 2:
         add(first_doc(0), cores, remain, 0)
-    if len(pieces) == 2:
-        add(doc, 1, pieces[:-1])
-    add(doc, 1, pieces[-1:])
+    joint = len(pieces) > 2
+    add(doc, 1, pieces[-1:] if joint else pieces)
     give_out(doc)
-    if cores == 2 and len(pieces) > 1:
-        add(mate(0, 1 - core), 1, pieces[:-1], 0)
     for h in range(1, chips):
         add(first_doc(h), cores, remain, h)
     if cores == 2:
-        add(mate(0, 1 - core), 1, pieces[-1:], 0)
+        add(mate(0, 1 - core), 1, pieces[1:] if joint else pieces, 0)
         give_out(mate(0, 1 - core))
     for h in range(1, chips):
-        if len(pieces) > 1:
-            add(first_doc(h), cores, pieces[:-1], h)
-        add(first_doc(h), cores, pieces[-1:], h)
+        if joint:
+            add(first_doc(h), cores, pieces[:1], h)
+        add(first_doc(h), cores, pieces[1:] if joint else pieces, h)
         for i in range(cores):
             give_out(first_doc(h) + i)
 

time: 39.5 us -> 38.5 us (0.975)
  Pallas kernels: 38.7 us -> 37.8 us
    pallas_call x1, Pallas kernels: 38.7 us -> 37.8 us  [shards(): pl.pallas_call(functools.partial(encode_kernel, (docs, vocs), count, tile...]
where the time goes in v6:
time: 38.5 us; the launch traced here: 38.4 us
  Pallas kernels  37.8 us (98%)
  local copies, waits for them, and re-layouts  0.6 us (2%)
    pallas_call x1, Pallas kernels, shards(): pl.pallas_call(functools.partial(encode_kernel, (docs, vocs), count, tile...  37.8 us

profile of v6, /device:TPU:2, one launch (start us, length us, event | category | flops | bytes accessed | tf_op | source)
XLA Modules:
  0.0 38.4 jit_solution(6009494840602394075)
XLA Ops:
  0.0 37.8 %shard_map.100 = f32[6,256]{1,0:T(8,128)S(1)} custom-call(s32[6]{0:T(128)} %lens.1, f32[768]{0:T(1024)} %b_trans.1, f32[768]{0:T(1024)} %gain.1, f32[768]{0:T(1024)} %bias.1, f32[7680]{0:T(1024)} %b_decode.1, bf16[1536,768]{1,0:T(8,128)(2,1)} %bitcast.3, bf16[768,768]{1,0:T(8,128)(2,1)} %w_trans.1, bf16[768,7680]{1,0:T(8,128)(2,1)} %w_decode.1, ...), custom_call_target="tpu_custom_call" | custom-call | tf_op jit(solution)/shard_map/pallas_call | solution.py:320
  37.8 0.6 %copy.12 = f32[6,256]{1,0:T(8,128)} copy(f32[6,256]{1,0:T(8,128)S(1)} %shard_map.100) | data formatting | bytes 12288

commit v7 on v6

--- a/solution.py
+++ b/solution.py
@@ -215,10 +215,11 @@
         begin += size
     part[...] = jnp.zeros_like(part)
 
-    def add_all(cut):
-        for h in range(chips):
-            arrive(h, cut)
-        part[...] += contract(pl.ds(0, docs), docs, [cut])
+    def add_all(cuts):
+        for cut in cuts:
+            for h in range(chips):
+                arrive(h, cut)
+        part[...] += contract(pl.ds(0, docs), docs, cuts)
 
     def first_doc(h):
         return cores * lax.rem(chip + chips - h, chips)
@@ -247,8 +248,11 @@
             pl.semaphore_wait(barrier, len(peers) + len(along))
         for i, cut in enumerate(whole_tiles[t:t + 1] or pieces):
             between = None
-            if t >= max(2, early) and i == 0:
-                between = functools.partial(add_all, whole_tiles[t - max(2, early)])
+            late = t - max(2, early)
+            if i == 0 and late >= 0 and (late % 2 or t == tiles - 1):
+                between = functools.partial(
+                    add_all, whole_tiles[late - late % 2 if late % 2 else late:late + 1]
+                )
             if t == tiles - 1 and i == 1:
                 between = functools.partial(add, first_doc(0), cores, remain, 0)
             if t == tiles - 1 and i == 2:
@@ -283,9 +287,12 @@
     for h in range(1, chips):
         if joint:
             add(first_doc(h), cores, pieces[:1], h)
-        add(first_doc(h), cores, pieces[1:] if joint else pieces, h)
-        for i in range(cores):
-            give_out(first_doc(h) + i)
+        last = pieces[1:] if joint else pieces
+        for j, (target, source) in enumerate(links[h]):
+            for cut in last:
+                share_copy(first_link[h] + j, target, cut).wait()
+            add(source, 1, last)
+            give_out(source)
 
     result = part[pl.ds(voc * share, share)]
     for j, peer in enumerate(along):

time: 38.5 us -> 38.3 us (level)
  no operation moved by 1% of the time
where the time goes in v7:
time: 38.3 us; the launch traced here: 38.1 us
  Pallas kernels  37.5 us (98%)
  local copies, waits for them, and re-layouts  0.6 us (2%)
    pallas_call x1, Pallas kernels, shards(): pl.pallas_call(functools.partial(encode_kernel, (docs, vocs), count, tile...  37.5 us

profile of v7, /device:TPU:2, one launch (start us, length us, event | category | flops | bytes accessed | tf_op | source)
XLA Modules:
  0.0 38.1 jit_solution(14269246553983339565)
XLA Ops:
  0.0 37.5 %shard_map.100 = f32[6,256]{1,0:T(8,128)S(1)} custom-call(s32[6]{0:T(128)} %lens.1, f32[768]{0:T(1024)} %b_trans.1, f32[768]{0:T(1024)} %gain.1, f32[768]{0:T(1024)} %bias.1, f32[7680]{0:T(1024)} %b_decode.1, bf16[1536,768]{1,0:T(8,128)(2,1)} %bitcast.3, bf16[768,768]{1,0:T(8,128)(2,1)} %w_trans.1, bf16[768,7680]{1,0:T(8,128)(2,1)} %w_decode.1, ...), custom_call_target="tpu_custom_call" | custom-call | tf_op jit(solution)/shard_map/pallas_call | solution.py:327
  37.5 0.6 %copy.12 = f32[6,256]{1,0:T(8,128)} copy(f32[6,256]{1,0:T(8,128)S(1)} %shard_map.100) | data formatting | bytes 12288

commit v8 on v7

--- a/solution.py
+++ b/solution.py
@@ -280,13 +280,11 @@
     add(doc, 1, pieces[-1:] if joint else pieces)
     give_out(doc)
     for h in range(1, chips):
-        add(first_doc(h), cores, remain, h)
+        add(first_doc(h), cores, remain + pieces[:1] if joint else remain, h)
     if cores == 2:
         add(mate(0, 1 - core), 1, pieces[1:] if joint else pieces, 0)
         give_out(mate(0, 1 - core))
     for h in range(1, chips):
-        if joint:
-            add(first_doc(h), cores, pieces[:1], h)
         last = pieces[1:] if joint else pieces
         for j, (target, source) in enumerate(links[h]):
             for cut in last:

time: 38.3 us -> 38.2 us (level)
  no operation moved by 1% of the time
where the time goes in v8:
time: 38.2 us; the launch traced here: 38 us
  Pallas kernels  37.4 us (98%)
  local copies, waits for them, and re-layouts  0.6 us (2%)
    pallas_call x1, Pallas kernels, shards(): pl.pallas_call(functools.partial(encode_kernel, (docs, vocs), count, tile...  37.4 us

profile of v8, /device:TPU:2, one launch (start us, length us, event | category | flops | bytes accessed | tf_op | source)
XLA Modules:
  0.0 38.0 jit_solution(6013613664315824651)
XLA Ops:
  0.0 37.4 %shard_map.100 = f32[6,256]{1,0:T(8,128)S(1)} custom-call(s32[6]{0:T(128)} %lens.1, f32[768]{0:T(1024)} %b_trans.1, f32[768]{0:T(1024)} %gain.1, f32[768]{0:T(1024)} %bias.1, f32[7680]{0:T(1024)} %b_decode.1, bf16[1536,768]{1,0:T(8,128)(2,1)} %bitcast.3, bf16[768,768]{1,0:T(8,128)(2,1)} %w_trans.1, bf16[768,7680]{1,0:T(8,128)(2,1)} %w_decode.1, ...), custom_call_target="tpu_custom_call" | custom-call | tf_op jit(solution)/shard_map/pallas_call | solution.py:325
  37.4 0.6 %copy.12 = f32[6,256]{1,0:T(8,128)} copy(f32[6,256]{1,0:T(8,128)S(1)} %shard_map.100) | data formatting | bytes 12288
